TPU v7x, 32 devices: a whole 2x2x4 slice. The times are simulated.
32 devices in a mesh: shard: 4 (over y, core), rep: 8 (over z, x).
Axes of the slice: x: 2, y: 2, z: 4, core: 2. Of those that a mesh axis runs over, the one named last changes fastest.
Arguments:
- block_input: bfloat16 [4096, 1024], P(('shard', 'rep')), may hold values from -6 to 6
- segments: int32 [4096], P(('shard', 'rep')), may hold values from 0 to 95, never falling along the last dimension, each value on 1 to 96 neighbouring positions
- cotangent: bfloat16 [4096, 1024], P(('shard', 'rep')), may hold values from -6 to 6
- gain_in: float32 [1024], replicated, may hold values from 0.5 to 1.5
- w_query: bfloat16 [1024, 768], P('shard'), may hold values from -0.1875 to 0.1875
- w_key: bfloat16 [1024, 768], P('shard'), may hold values from -0.1875 to 0.1875
- w_value: bfloat16 [1024, 1536], P('shard'), may hold values from -0.1875 to 0.1875
- conv_q: float32 [4, 768], replicated, may hold values from -3 to 3
- conv_k: float32 [4, 768], replicated, may hold values from -3 to 3
- conv_v: float32 [4, 1536], replicated, may hold values from -3 to 3
- w_decay: bfloat16 [1024, 6], replicated, may hold values from -0.1875 to 0.1875
- w_beta: bfloat16 [1024, 6], replicated, may hold values from -0.1875 to 0.1875
- a_log: float32 [6], replicated, may hold values from -3 to 0.5
- dt_bias: float32 [6], replicated, may hold values from -3 to -1
- w_gate_out: bfloat16 [1024, 1536], P('shard'), may hold values from -0.1875 to 0.1875
- gain_o: float32 [256], replicated, may hold values from 0.5 to 1.5
- w_out: bfloat16 [1536, 1024], P('shard'), may hold values from -0.3125 to 0.3125
- gain_mid: float32 [1024], replicated, may hold values from 0.5 to 1.5
- w_ffgate: bfloat16 [1024, 2816], P('shard'), may hold values from -0.1875 to 0.1875
- w_ffup: bfloat16 [1024, 2816], P('shard'), may hold values from -0.1875 to 0.1875
- w_down: bfloat16 [2816, 1024], P('shard'), may hold values from -0.21875 to 0.21875
Outputs:
- block_output: bfloat16 [4096, 1024], P(('shard', 'rep'))
- d_input: float32 [4096, 1024], P(('shard', 'rep'))
- d_gain_in: float32 [1024], replicated
- d_query: float32 [1024, 768], P('shard', 'rep')
- d_key: float32 [1024, 768], P('shard', 'rep')
- d_value: float32 [1024, 1536], P('shard', 'rep')
- d_conv_q: float32 [4, 768], replicated
- d_conv_k: float32 [4, 768], replicated
- d_conv_v: float32 [4, 1536], replicated
- d_decay: float32 [1024, 6], replicated
- d_beta: float32 [1024, 6], replicated
- d_a_log: float32 [6], replicated
- d_dt_bias: float32 [6], replicated
- d_gate_out: float32 [1024, 1536], P('shard', 'rep')
- d_gain_o: float32 [256], replicated
- d_out: float32 [1536, 1024], P('shard', 'rep')
- d_gain_mid: float32 [1024], replicated
- d_ffgate: float32 [1024, 2816], P('shard', 'rep')
- d_ffup: float32 [1024, 2816], P('shard', 'rep')
- d_down: float32 [2816, 1024], P('shard', 'rep')
Inputs may be any that keep to these rules, and one draw needn't show every extreme that they name: `segments`: document numbers never fall along the tokens; a document covers 1 to (96) tokens, and one covers exactly that many.
All inputs are finite; a program needn't handle non-finite values.
Results may differ from a plain program's by a relative error of at most 0.017.
The roundings to bfloat16 on the way count: a program that leaves them out, or rounds other values in their place, can miss the bound.
Values may be sent and summed in bfloat16 or wider, within the bound.
No kernel may reach another device: no remote copies, remote signals or barrier semaphores. Data moves between devices by JAX's collectives and lax.ppermute only.
A program may use at most 192 MiB of HBM per device.

v0:
```python
from functools import partial
import jax
import jax.numpy as jnp
from jax import lax
from jax.sharding import PartitionSpec as P

SPAN = 64
SEQ = 128


def norm_apply(hidden, gain):
    return hidden * lax.rsqrt(jnp.mean(hidden * hidden, axis=-1, keepdims=True) + 1e-05) * gain


def causal_conv(stream, taps, same_list):
    total = stream * taps[0]
    for lag in range(1, taps.shape[0]):
        moved = jnp.pad(stream, ((0, 0), (lag, 0), (0, 0)))[:, : stream.shape[1]]
        total = total + moved * taps[lag] * same_list[lag][:, :, None]
    return jax.nn.silu(total)


def unit_heads(stream, heads):
    batch, length, width = stream.shape
    split = stream.reshape(batch, length, heads, width // heads)
    return split * lax.rsqrt(jnp.sum(split * split, axis=-1, keepdims=True) + 1e-06)


def to_blocks(array, batch, blocks):
    shaped = array.reshape((batch, blocks, SPAN) + array.shape[2:])
    return jnp.moveaxis(jnp.moveaxis(shaped, 1, 0), 2, 3)


def mixer(seg, qp, kp, vp, zp, decay_raw, beta_raw, conv_q, conv_k, conv_v, a_log, dt_bias, gain_o):
    batch, length = seg.shape
    heads = a_log.shape[0]
    highest = lax.Precision.HIGHEST
    same_list = []
    for lag in range(conv_q.shape[0]):
        earlier = jnp.pad(seg, ((0, 0), (lag, 0)), constant_values=-1)[:, :length]
        same_list.append((earlier == seg).astype(jnp.float32))
    query = unit_heads(causal_conv(qp, conv_q, same_list), heads)
    query = query * query.shape[-1] ** (-0.5)
    keys = unit_heads(causal_conv(kp, conv_k, same_list), heads)
    value = causal_conv(vp, conv_v, same_list)
    value = value.reshape(batch, length, heads, value.shape[-1] // heads)
    log_decay = -jnp.exp(a_log) * jax.nn.softplus(decay_raw + dt_bias)
    beta = jax.nn.sigmoid(beta_raw)
    blocks = length // SPAN
    query_b = to_blocks(query, batch, blocks)
    keys_b = to_blocks(keys, batch, blocks)
    value_b = to_blocks(value, batch, blocks)
    decay_b = to_blocks(log_decay, batch, blocks)
    beta_b = to_blocks(beta, batch, blocks)
    seg_b = jnp.moveaxis(seg.reshape(batch, blocks, SPAN), 1, 0)
    seg_prev = jnp.concatenate([jnp.full((1, batch), -1, seg.dtype), seg_b[:-1, :, -1]], axis=0)
    identity = jnp.eye(SPAN, dtype=jnp.float32)
    lower = jnp.tril(jnp.ones((SPAN, SPAN), jnp.float32))
    width_v = value.shape[-1]

    def span_step(state, items):
        qc, kc, vc, gc, bc, sc, sp = items
        cum = jnp.cumsum(gc, axis=-1)
        same = (sc[:, :, None] == sc[:, None, :]).astype(jnp.float32) * lower
        decay = jnp.exp(jnp.minimum(cum[..., :, None] - cum[..., None, :], 0.0)) * same[:, None]
        enter = jnp.exp(cum) * (sc == sp[:, None]).astype(jnp.float32)[:, None, :]
        inner = jnp.einsum("bhtd,bhsd->bhts", kc, kc, precision=highest)
        system = identity + bc[..., :, None] * decay * (1.0 - identity) * inner
        rhs = jnp.concatenate([bc[..., None] * vc, (bc * enter)[..., None] * kc], axis=-1)
        solved = jax.scipy.linalg.solve_triangular(system, rhs, lower=True, unit_diagonal=True)
        fresh = solved[..., :width_v] - jnp.einsum(
            "bhtk,bhkv->bhtv", solved[..., width_v:], state, precision=highest
        )
        scores = jnp.einsum("bhtd,bhsd->bhts", qc, kc, precision=highest) * decay
        result = enter[..., None] * jnp.einsum("bhtk,bhkv->bhtv", qc, state, precision=highest)
        result = result + jnp.einsum("bhts,bhsv->bhtv", scores, fresh, precision=highest)
        weighted = decay[..., -1, :][..., None] * kc
        new_state = enter[..., -1][..., None, None] * state + jnp.einsum(
            "bhsk,bhsv->bhkv", weighted, fresh, precision=highest
        )
        return (new_state, result)

    start = jnp.zeros((batch, heads, keys.shape[-1], width_v), jnp.float32)
    _, outs = lax.scan(
        span_step, start, (query_b, keys_b, value_b, decay_b, beta_b, seg_b, seg_prev)
    )
    core = jnp.moveaxis(jnp.moveaxis(outs, 3, 2), 0, 1).reshape(batch, length, heads, width_v)
    gated = core * lax.rsqrt(jnp.mean(core * core, axis=-1, keepdims=True) + 1e-05) * gain_o
    gated = gated * jax.nn.silu(zp.reshape(batch, length, heads, width_v))
    return gated.reshape(batch, length, heads * width_v)


def dot_plain(left, right):
    return jnp.dot(left, right, preferred_element_type=jnp.float32)


def dot_trans(left, right):
    return lax.dot_general(
        left, right, (((1,), (1,)), ((), ())), preferred_element_type=jnp.float32
    )


def dot_outer(left, right):
    return lax.dot_general(
        left, right, (((0,), (0,)), ((), ())), preferred_element_type=jnp.float32
    )


def keep_pair(left, right):
    return (left, right)


def forward_pass(tokens_in, segments, large, small):
    w_query, w_key, w_value, w_gate_out, w_out, w_ffgate, w_ffup, w_down = large
    gain_in, gain_mid, conv_q, conv_k, conv_v, w_decay, w_beta, a_log, dt_bias, gain_o = small
    rows = tokens_in.shape[0]
    batch = rows // SEQ
    seg = segments.reshape(batch, SEQ)
    resid = tokens_in.astype(jnp.float32)
    normed = norm_apply(resid, gain_in).astype(jnp.bfloat16)
    inputs = tuple(
        (
            dot_plain(normed, weight)
            for weight in (w_query, w_key, w_value, w_gate_out, w_decay, w_beta)
        )
    )
    shaped = tuple((item.reshape(batch, SEQ, item.shape[-1]) for item in inputs))
    mixed = (
        mixer(seg, *shaped, conv_q, conv_k, conv_v, a_log, dt_bias, gain_o)
        .reshape(rows, -1)
        .astype(jnp.bfloat16)
    )
    hidden1 = resid + dot_plain(mixed, w_out)
    normed2 = norm_apply(hidden1, gain_mid).astype(jnp.bfloat16)
    gate = dot_plain(normed2, w_ffgate)
    up = dot_plain(normed2, w_ffup)
    act = (jax.nn.silu(gate) * up).astype(jnp.bfloat16)
    output = (hidden1 + dot_plain(act, w_down)).astype(jnp.bfloat16)
    saved = (resid, normed, shaped, seg, mixed, hidden1, normed2, gate, up, act)
    return (saved, output)


def backward_ffn(saved, cotangent, large, small, outer):
    resid, normed, shaped, seg, mixed, hidden1, normed2, gate, up, act = saved
    w_ffgate, w_ffup, w_down = (large[5], large[6], large[7])
    gain_mid = small[1]
    g_down = outer(act, cotangent)
    d_act = dot_trans(cotangent, w_down)
    sig = jax.nn.sigmoid(gate)
    d_gate = (d_act * up * sig * (1.0 + gate * (1.0 - sig))).astype(jnp.bfloat16)
    d_up = (d_act * gate * sig).astype(jnp.bfloat16)
    g_ffgate = outer(normed2, d_gate)
    g_ffup = outer(normed2, d_up)
    d_normed2 = dot_trans(d_gate, w_ffgate) + dot_trans(d_up, w_ffup)
    _, pull = jax.vjp(norm_apply, hidden1, gain_mid)
    d_from_norm, g_gain_mid = pull(d_normed2)
    d_hidden1 = cotangent.astype(jnp.float32) + d_from_norm
    return (d_hidden1, (g_ffgate, g_ffup, g_down), g_gain_mid)


def backward_mixer(saved, d_hidden1, large, small, outer):
    resid, normed, shaped, seg, mixed, hidden1, normed2, gate, up, act = saved
    w_query, w_key, w_value, w_gate_out, w_out = large[:5]
    gain_in, gain_mid, conv_q, conv_k, conv_v, w_decay, w_beta, a_log, dt_bias, gain_o = small
    rows = resid.shape[0]
    d_hidden_b = d_hidden1.astype(jnp.bfloat16)
    g_out = outer(mixed, d_hidden_b)
    d_mixed = dot_trans(d_hidden_b, w_out)
    _, pull = jax.vjp(partial(mixer, seg), *shaped, conv_q, conv_k, conv_v, a_log, dt_bias, gain_o)
    grads = pull(d_mixed.reshape(shaped[2].shape[0], SEQ, -1))
    flat = tuple((item.reshape(rows, -1).astype(jnp.bfloat16) for item in grads[:6]))
    weights = (w_query, w_key, w_value, w_gate_out, w_decay, w_beta)
    g_proj = tuple((outer(normed, item) for item in flat[:4]))
    g_decay = dot_outer(normed, flat[4])
    g_beta = dot_outer(normed, flat[5])
    d_normed = dot_trans(flat[0], weights[0])
    for item, weight in zip(flat[1:], weights[1:]):
        d_normed = d_normed + dot_trans(item, weight)
    _, pull_in = jax.vjp(norm_apply, resid, gain_in)
    d_from_norm, g_gain_in = pull_in(d_normed)
    d_input = d_hidden1 + d_from_norm
    large_grads = (g_proj[0], g_proj[1], g_proj[2], g_proj[3], g_out)
    small_grads = (
        g_gain_in,
        grads[6],
        grads[7],
        grads[8],
        g_decay,
        g_beta,
        grads[9],
        grads[10],
        grads[11],
    )
    return (d_input, large_grads, small_grads)


def owned_columns(left, count, index):
    width = left.shape[1] // count
    return lax.dynamic_slice_in_dim(left, index * width, width, 1)


def body(
    block_input,
    segments,
    cotangent,
    gain_in,
    w_query,
    w_key,
    w_value,
    conv_q,
    conv_k,
    conv_v,
    w_decay,
    w_beta,
    a_log,
    dt_bias,
    w_gate_out,
    gain_o,
    w_out,
    gain_mid,
    w_ffgate,
    w_ffup,
    w_down,
):
    small = (gain_in, gain_mid, conv_q, conv_k, conv_v, w_decay, w_beta, a_log, dt_bias, gain_o)
    gathered = (
        lax.all_gather(w_query, "shard", axis=0, tiled=True),
        lax.all_gather(w_key, "shard", axis=0, tiled=True),
        lax.all_gather(w_value, "shard", axis=0, tiled=True),
        lax.all_gather(w_gate_out, "shard", axis=0, tiled=True),
        lax.all_gather(w_out, "shard", axis=0, tiled=True),
        lax.all_gather(w_ffgate, "shard", axis=0, tiled=True),
        lax.all_gather(w_ffup, "shard", axis=0, tiled=True),
        lax.all_gather(w_down, "shard", axis=0, tiled=True),
    )
    saved, output = forward_pass(block_input, segments, gathered, small)
    d_hidden1, ffn_pairs, g_gain_mid = backward_ffn(saved, cotangent, gathered, small, keep_pair)
    d_input, mix_pairs, mix_small = backward_mixer(saved, d_hidden1, gathered, small, keep_pair)
    factors = (
        lax.all_gather(mix_pairs[0][0], "shard", axis=0, tiled=True),
        lax.all_gather(mix_pairs[4][0], "shard", axis=0, tiled=True),
        lax.all_gather(ffn_pairs[0][0], "shard", axis=0, tiled=True),
        lax.all_gather(ffn_pairs[2][0], "shard", axis=0, tiled=True),
        lax.all_gather(mix_pairs[0][1], "shard", axis=0, tiled=True),
        lax.all_gather(mix_pairs[1][1], "shard", axis=0, tiled=True),
        lax.all_gather(mix_pairs[2][1], "shard", axis=0, tiled=True),
        lax.all_gather(mix_pairs[3][1], "shard", axis=0, tiled=True),
        lax.all_gather(mix_pairs[4][1], "shard", axis=0, tiled=True),
        lax.all_gather(ffn_pairs[0][1], "shard", axis=0, tiled=True),
        lax.all_gather(ffn_pairs[1][1], "shard", axis=0, tiled=True),
        lax.all_gather(ffn_pairs[2][1], "shard", axis=0, tiled=True),
    )
    count = lax.axis_size("shard")
    index = lax.axis_index("shard")
    normed_own = owned_columns(factors[0], count, index)
    mixed_own = owned_columns(factors[1], count, index)
    normed2_own = owned_columns(factors[2], count, index)
    act_own = owned_columns(factors[3], count, index)
    own_rows = (
        dot_outer(normed_own, factors[4]),
        dot_outer(normed_own, factors[5]),
        dot_outer(normed_own, factors[6]),
        dot_outer(normed_own, factors[7]),
        dot_outer(mixed_own, factors[8]),
        dot_outer(normed2_own, factors[9]),
        dot_outer(normed2_own, factors[10]),
        dot_outer(act_own, factors[11]),
    )
    large_final = (
        lax.psum_scatter(own_rows[0], "rep", scatter_dimension=1, tiled=True),
        lax.psum_scatter(own_rows[1], "rep", scatter_dimension=1, tiled=True),
        lax.psum_scatter(own_rows[2], "rep", scatter_dimension=1, tiled=True),
        lax.psum_scatter(own_rows[3], "rep", scatter_dimension=1, tiled=True),
        lax.psum_scatter(own_rows[4], "rep", scatter_dimension=1, tiled=True),
        lax.psum_scatter(own_rows[5], "rep", scatter_dimension=1, tiled=True),
        lax.psum_scatter(own_rows[6], "rep", scatter_dimension=1, tiled=True),
        lax.psum_scatter(own_rows[7], "rep", scatter_dimension=1, tiled=True),
    )
    small_terms = (mix_small[0], g_gain_mid) + tuple(mix_small[1:])
    small_final = lax.psum(
        (
            small_terms[0],
            small_terms[1],
            small_terms[2],
            small_terms[3],
            small_terms[4],
            small_terms[5],
            small_terms[6],
            small_terms[7],
            small_terms[8],
            small_terms[9],
        ),
        ("shard", "rep"),
    )
    g_query, g_key, g_value, g_gate_out, g_out, g_ffgate, g_ffup, g_down = large_final
    (
        g_gain_in,
        g_gain_mid2,
        g_conv_q,
        g_conv_k,
        g_conv_v,
        g_decay,
        g_beta,
        g_a_log,
        g_dt_bias,
        g_gain_o,
    ) = small_final
    return (
        output,
        d_input,
        g_gain_in,
        g_query,
        g_key,
        g_value,
        g_conv_q,
        g_conv_k,
        g_conv_v,
        g_decay,
        g_beta,
        g_a_log,
        g_dt_bias,
        g_gate_out,
        g_gain_o,
        g_out,
        g_gain_mid2,
        g_ffgate,
        g_ffup,
        g_down,
    )


def solution(mesh):
    return jax.shard_map(
        body,
        mesh=mesh,
        in_specs=(
            P(("shard", "rep"), None),
            P(("shard", "rep")),
            P(("shard", "rep"), None),
            P(),
            P("shard", None),
            P("shard", None),
            P("shard", None),
            P(),
            P(),
            P(),
            P(),
            P(),
            P(),
            P(),
            P("shard", None),
            P(),
            P("shard", None),
            P(),
            P("shard", None),
            P("shard", None),
            P("shard", None),
        ),
        out_specs=(
            P(("shard", "rep"), None),
            P(("shard", "rep"), None),
            P(),
            P("shard", "rep"),
            P("shard", "rep"),
            P("shard", "rep"),
            P(),
            P(),
            P(),
            P(),
            P(),
            P(),
            P(),
            P("shard", "rep"),
            P(),
            P("shard", "rep"),
            P(),
            P("shard", "rep"),
            P("shard", "rep"),
            P("shard", "rep"),
        ),
        check_vma=False,
    )
```

profile of v0, /device:TPU:0, one launch (start us, length us, event | category | flops | bytes accessed | tf_op | source)
XLA Modules:
  0.0 1416.3 jit_solution(15208728799947843738)
XLA Ops:
  22.7 9.3 all-gather.26.cloned.1.call-done
  32.0 1.9 fusion.335
  33.9 19.4 %all-gather.22.cloned.1.call-done = bf16[1024,768]{1,0:T(8,128)(2,1)} async-done(((bf16[256,768]{1,0:T(8,128)(2,1)}), bf16[1024,768]{1,0:T(8,128)(2,1)}) %all-gather.22.cloned.1.call-update) | async-done | bytes 1572880 | tf_op jit(solution)/shard_map/all_gather | solution.py:228
  58.2 2.0 reshape.2186
  66.4 17.0 %all-gather.24.cloned.1.call-done = bf16[1024,1536]{1,0:T(8,128)(2,1)} async-done(((bf16[256,1536]{1,0:T(8,128)(2,1)}), bf16[1024,1536]{1,0:T(8,128)(2,1)}) %all-gather.24.cloned.1.call-update) | async-done | bytes 3145744 | tf_op jit(solution)/shard_map/all_gather | solution.py:229
  83.4 2.5 fusion.334
  87.8 2.3 reshape_reshape.12
  90.1 2.4 copy.216
  93.5 101.3 %while.103 = (s32[]{:T(128)}, f32[1,6,128,256]{3,2,1,0:T(8,128)S(1)}, f32[2,1,6,64,256]{4,3,2,1,0:T(8,128)}, f32[2,1,6,64]{3,2,1,0:T(8,128)}, s32[2,1,64]{2,1,0:...) while((s32[]{:T(128)}, ...), condition=%wide.region_5.7_spmd.clone.clone, body=%wide.region_3.6_spmd.clone.clone.sunk | while | flops 719243328 | bytes 16660529 | solution.py:84
  100.9 30.2 %custom-call.45 = f32[6,1,64,64]{2,3,1,0:T(8,128)S(1)} custom-call(f32[6,1,64,64]{3,2,1,0:T(8,128)} %fusion.510), custom_call_target="InvertDiagBlocksLowerTriangular" | custom-call | tf_op jit(solution)/shard_map/while/body/eval_jaxpr/jit(_solve_triangular)/vmap()/triangular_solve/custom-call.1 | solution.py:70
  151.5 30.2 %custom-call.45 = f32[6,1,64,64]{2,3,1,0:T(8,128)S(1)} custom-call(f32[6,1,64,64]{3,2,1,0:T(8,128)} %fusion.510), custom_call_target="InvertDiagBlocksLowerTriangular" | custom-call | tf_op jit(solution)/shard_map/while/body/eval_jaxpr/jit(_solve_triangular)/vmap()/triangular_solve/custom-call.1 | solution.py:70
  200.6 116.1 %while.104 = (s32[]{:T(128)}, f32[1,6,128,256]{3,2,1,0:T(8,128)S(1)}, f32[2,1,6,64,256]{4,3,2,1,0:T(8,128)}, f32[2,1,6,64,64]{4,3,2,1,0:T(8,128)}, f32[2,1,6,64,...) while((s32[]{:T(128)}, ...), condition=%wide.region_11.13_spmd.clone.clone, body=%wide.region_9.12_spmd.clone.clone.sunk | while | flops 719999424 | bytes 37368836 | solution.py:84
  208.5 30.1 %custom-call.46 = f32[6,1,64,64]{2,3,1,0:T(8,128)} custom-call(f32[6,1,64,64]{3,2,1,0:T(8,128)S(1)} %add_bitcast_fusion.5), custom_call_target="InvertDiagBlocksLowerTriangular" | custom-call | tf_op jit(solution)/shard_map/jvp()/while/body/eval_jaxpr/jit(_solve_triangular)/vmap()/triangular_solve/custom-call.1 | solution.py:70
  239.9 2.5 constant_dynamic-update-slice_fusion.20
  243.7 2.3 bitcast_dynamic-update-slice_fusion.21
  266.3 30.1 %custom-call.46 = f32[6,1,64,64]{2,3,1,0:T(8,128)} custom-call(f32[6,1,64,64]{3,2,1,0:T(8,128)S(1)} %add_bitcast_fusion.5), custom_call_target="InvertDiagBlocksLowerTriangular" | custom-call | tf_op jit(solution)/shard_map/jvp()/while/body/eval_jaxpr/jit(_solve_triangular)/vmap()/triangular_solve/custom-call.1 | solution.py:70
  297.7 2.4 constant_dynamic-update-slice_fusion.20
  301.5 2.4 bitcast_dynamic-update-slice_fusion.21
  326.0 4.0 multiply_convert_fusion.3
  331.5 2.7 multiply_reduce_fusion.8
  334.5 4.7 fusion.336
  339.2 5.0 fusion.337
  344.2 7.2 multiply_convert_fusion
  351.5 5.7 fusion.338
  357.1 5.6 multiply_reduce_fusion.6
  364.5 4.9 fusion.243
  369.4 2.4 reshape_reshape.13
  371.8 2.7 fusion.234
  377.3 2.0 fusion.230
  383.4 137.2 %while.102 = (s32[]{:T(128)}, f32[1,6,128,256]{2,3,1,0:T(8,128)S(1)}, f32[2,1,6,64,128]{4,3,2,1,0:T(8,128)}, f32[2,1,6,64,128]{4,3,0,2,1:T(8,128)}, f32[2,1,6,64...) while((s32[]{:T(128)}, ...), condition=%wide.region_24.26_spmd.clone, body=%wide.region_14.25_spmd.clone.sunk | while | flops 1457530112 | bytes 72648632 | solution.py:84
  383.5 2.0 convolution_bitcast_fusion.22
  389.5 30.9 %custom-call.44 = f32[6,1,64,64]{2,3,1,0:T(8,128)} custom-call(f32[6,1,64,64]{3,2,1,0:T(8,128)} %add_bitcast_fusion.4), custom_call_target="InvertDiagBlocksLowerTriangular" | custom-call | tf_op jit(solution)/shard_map/transpose(jvp())/while/body/eval_jaxpr/jit(_solve_triangular)/vmap()/triangular_solve | solution.py:70
  422.1 2.6 fusion.487
  428.9 2.7 fusion.488
  452.0 2.0 convolution_bitcast_fusion.22
  457.9 30.9 %custom-call.44 = f32[6,1,64,64]{2,3,1,0:T(8,128)} custom-call(f32[6,1,64,64]{3,2,1,0:T(8,128)} %add_bitcast_fusion.4), custom_call_target="InvertDiagBlocksLowerTriangular" | custom-call | tf_op jit(solution)/shard_map/transpose(jvp())/while/body/eval_jaxpr/jit(_solve_triangular)/vmap()/triangular_solve | solution.py:70
  490.6 2.6 fusion.487
  497.3 2.7 fusion.488
  522.6 2.5 multiply_reduce_fusion.4
  536.7 2.4 multiply_reduce_fusion.16
  552.9 11.8 all-gather.1
  564.7 2.3 fusion.244
  567.1 8.7 all-gather
  575.8 2.3 fusion.246
  578.3 3.2 fusion.280
  581.6 3.3 fusion.223
  585.3 3.3 fusion.291
  589.2 28.5 %all-gather.48.cloned.1.call-done = bf16[512,2816]{1,0:T(8,128)(2,1)} async-done(((bf16[128,2816]{1,0:T(8,128)(2,1)}), bf16[512,2816]{1,0:T(8,128)(2,1)}) %all-gather.48.cloned.1.call-update) | async-done | bytes 2883600 | tf_op jit(solution)/shard_map/all_gather | solution.py:249
  617.6 4.7 fusion.286
  622.5 23.7 %all-gather.50.cloned.1.call-done = bf16[512,2816]{1,0:T(8,128)(2,1)} async-done(((bf16[128,2816]{1,0:T(8,128)(2,1)}), bf16[512,2816]{1,0:T(8,128)(2,1)}) %all-gather.50.cloned.1.call-update) | async-done | bytes 2883600 | tf_op jit(solution)/shard_map/all_gather | solution.py:250
  646.1 4.8 fusion.284
  651.0 13.2 all-gather.54.cloned.1.call-done
  664.2 28.5 %all-gather.52.cloned.1.call-done = bf16[512,2816]{1,0:T(8,128)(2,1)} async-done(((bf16[128,2816]{1,0:T(8,128)(2,1)}), bf16[512,2816]{1,0:T(8,128)(2,1)}) %all-gather.52.cloned.1.call-update) | async-done | bytes 2883600 | tf_op jit(solution)/shard_map/all_gather | solution.py:243
  692.7 4.3 fusion.250
  699.4 4.3 fusion.226
  703.6 126.9 %all-reduce.40.cloned.1.call-done = (f32[1024]{0:T(1024)}, f32[4,768]{1,0:T(4,128)}, f32[4,768]{1,0:T(4,128)}, f32[4,1536]{1,0:T(4,128)}, f32[1024,6]{0,1:T(8,12...) async-done(((f32[1024]{0:T(1024)}, f32[4,768]{1,0:T(4,128)}, f32[4,768]{1,0:T(4,128)}, f32[4,1536]{1,0:T(4,128)}, ...) | async-done | bytes 107584 | tf_op jit(solution)/shard_map/psum | solution.py:280
  830.5 66.2 %reduce-scatter.11.cloned.1.call-done = f32[256,96]{0,1:T(8,128)} async-done(((f32[256,768]{0,1:T(8,128)}), f32[256,96]{0,1:T(8,128)}) %reduce-scatter.11.cloned.1.call-update) | async-done | bytes 98320 | tf_op jit(solution)/shard_map/reduce_scatter | solution.py:271
  896.7 66.2 %reduce-scatter.9.cloned.1.call-done = f32[256,96]{0,1:T(8,128)} async-done(((f32[256,768]{0,1:T(8,128)}), f32[256,96]{0,1:T(8,128)}) %reduce-scatter.9.cloned.1.call-update) | async-done | bytes 98320 | tf_op jit(solution)/shard_map/reduce_scatter | solution.py:270
  962.9 69.6 %reduce-scatter.17.cloned.1.call-done = f32[384,128]{1,0:T(8,128)} async-done(((f32[384,1024]{1,0:T(8,128)}), f32[384,128]{1,0:T(8,128)}) %reduce-scatter.17.cloned.1.call-update) | async-done | bytes 196624 | tf_op jit(solution)/shard_map/reduce_scatter | solution.py:274
  1032.6 68.6 %reduce-scatter.13.cloned.1.call-done = f32[256,192]{0,1:T(8,128)} async-done(((f32[256,1536]{0,1:T(8,128)}), f32[256,192]{0,1:T(8,128)}) %reduce-scatter.13.cloned.1.call-update) | async-done | bytes 196624 | tf_op jit(solution)/shard_map/reduce_scatter | solution.py:272
  1101.1 68.4 %reduce-scatter.15.cloned.1.call-done = f32[256,192]{0,1:T(8,128)} async-done(((f32[256,1536]{0,1:T(8,128)}), f32[256,192]{0,1:T(8,128)}) %reduce-scatter.15.cloned.1.call-update) | async-done | bytes 196624 | tf_op jit(solution)/shard_map/reduce_scatter | solution.py:273
  1169.6 75.4 %reduce-scatter.19.cloned.1.call-done = f32[256,352]{0,1:T(8,128)} async-done(((f32[256,2816]{0,1:T(8,128)}), f32[256,352]{0,1:T(8,128)}) %reduce-scatter.19.cloned.1.call-update) | async-done | bytes 360464 | tf_op jit(solution)/shard_map/reduce_scatter | solution.py:275
  1245.0 75.5 %reduce-scatter.21.cloned.1.call-done = f32[256,352]{0,1:T(8,128)} async-done(((f32[256,2816]{0,1:T(8,128)}), f32[256,352]{0,1:T(8,128)}) %reduce-scatter.21.cloned.1.call-update) | async-done | bytes 360464 | tf_op jit(solution)/shard_map/reduce_scatter | solution.py:276
  1320.4 76.0 %reduce-scatter.23.cloned.1.call-done = f32[704,128]{1,0:T(8,128)} async-done(((f32[704,1024]{1,0:T(8,128)}), f32[704,128]{1,0:T(8,128)}) %reduce-scatter.23.cloned.1.call-update) | async-done | bytes 360464 | tf_op jit(solution)/shard_map/reduce_scatter | solution.py:277
  (986 shorter events, 241.1 us)
Async XLA Ops:
  7.2 9.7 copy-start
  7.2 24.8 %all-gather.26.cloned.1.call-start = ((), (), s32[]{:S(2)}) async-start(), calls=%async_computation.10 | async-start | bytes 1966080 | tf_op jit(solution)/shard_map/all_gather | solution.py:227
  7.9 45.4 %all-gather.22.cloned.1.call-start = ((), (), s32[]{:S(2)}) async-start(), calls=%async_computation.8 | async-start | bytes 1966080 | tf_op jit(solution)/shard_map/all_gather | solution.py:228
  8.7 74.7 %all-gather.24.cloned.1.call-start = ((), (), s32[]{:S(2)}) async-start(), calls=%async_computation.9 | async-start | bytes 3932160 | tf_op jit(solution)/shard_map/all_gather | solution.py:229
  9.4 316.5 %all-gather.28.cloned.1.call-start = ((), (), s32[]{:S(2)}) async-start(), calls=%async_computation.11 | async-start | bytes 3932160 | tf_op jit(solution)/shard_map/all_gather | solution.py:230
  10.0 321.5 %all-gather.30.cloned.1.call-start = ((), (), s32[]{:S(2)}) async-start(), calls=%async_computation.12 | async-start | bytes 3932160 | tf_op jit(solution)/shard_map/all_gather | solution.py:231
  10.6 323.9 %all-gather.32.cloned.1.call-start = ((), (), s32[]{:S(2)}) async-start(), calls=%async_computation.13 | async-start | bytes 7208960 | tf_op jit(solution)/shard_map/all_gather | solution.py:232
  11.2 328.0 %all-gather.34.cloned.1.call-start = ((), (), s32[]{:S(2)}) async-start(), calls=%async_computation.14 | async-start | bytes 7208960 | tf_op jit(solution)/shard_map/all_gather | solution.py:233
  12.0 8.6 copy-start.177
  12.0 9.9 copy-start.175
  12.0 9.9 copy-start.176
  12.0 332.2 %all-gather.36.cloned.1.call-start = ((), (), s32[]{:S(2)}) async-start(), calls=%async_computation.15 | async-start | bytes 7208960 | tf_op jit(solution)/shard_map/all_gather | solution.py:234
  12.8 552.0 %all-gather.38.cloned.1.call-start = ((), (), s32[]{:S(2)}) async-start(), calls=%async_computation.16 | async-start | bytes 1310720 | tf_op jit(solution)/shard_map/all_gather | solution.py:240
  13.9 39.4 %copy-start.24 = (bf16[128,1024]{1,0:T(8,128)(2,1)S(1)}, bf16[128,1024]{1,0:T(8,128)(2,1)}, u32[]{:S(2)}) copy-start(bf16[128,1024]{1,0:T(8,128)(2,1)} %fusion.255) | copy-start | bytes 786436
  13.9 564.4 %all-gather.42.cloned.1.call-start = ((), (), s32[]{:S(2)}) async-start(), calls=%async_computation.22 | async-start | bytes 1966080 | tf_op jit(solution)/shard_map/all_gather | solution.py:241
  14.9 71.0 %copy-start.163 = (f32[128]{0:T(128)}, f32[128]{0:T(128)S(1)}, u32[]{:S(2)}) copy-start(f32[128]{0:T(128)S(1)} %get-tuple-element.2165) | copy-start | bytes 1540
  14.9 71.0 %copy-start.166 = (f32[128]{0:T(128)}, f32[128]{0:T(128)S(1)}, u32[]{:S(2)}) copy-start(f32[128]{0:T(128)S(1)} %get-tuple-element.2166) | copy-start | bytes 1540
  14.9 71.0 %copy-start.169 = (f32[128]{0:T(128)}, f32[128]{0:T(128)S(1)}, u32[]{:S(2)}) copy-start(f32[128]{0:T(128)S(1)} %get-tuple-element.2167) | copy-start | bytes 1540
  15.0 71.0 %copy-start.106 = (f32[1536]{0:T(1024)}, f32[1536]{0:T(1024)S(1)}, u32[]{:S(2)}) copy-start(f32[1536]{0:T(1024)S(1)} %get-tuple-element.1907) | copy-start | bytes 18436
  15.0 71.0 %copy-start.108 = (f32[1536]{0:T(1024)}, f32[1536]{0:T(1024)S(1)}, u32[]{:S(2)}) copy-start(f32[1536]{0:T(1024)S(1)} %get-tuple-element.1908) | copy-start | bytes 18436
  15.0 71.0 %copy-start.110 = (f32[1536]{0:T(1024)}, f32[1536]{0:T(1024)S(1)}, u32[]{:S(2)}) copy-start(f32[1536]{0:T(1024)S(1)} %get-tuple-element.1909) | copy-start | bytes 18436
  15.0 71.0 %copy-start.112 = (f32[1536]{0:T(1024)}, f32[1536]{0:T(1024)S(1)}, u32[]{:S(2)}) copy-start(f32[1536]{0:T(1024)S(1)} %get-tuple-element.1910) | copy-start | bytes 18436
  22.0 33.1 %copy-start.131 = (f32[768]{0:T(1024)}, f32[768]{0:T(1024)S(1)}, u32[]{:S(2)}) copy-start(f32[768]{0:T(1024)S(1)} %get-tuple-element.1911) | copy-start | bytes 9220
  22.0 33.1 %copy-start.133 = (f32[768]{0:T(1024)}, f32[768]{0:T(1024)S(1)}, u32[]{:S(2)}) copy-start(f32[768]{0:T(1024)S(1)} %get-tuple-element.2181) | copy-start | bytes 9220
  22.0 33.1 %copy-start.135 = (f32[768]{0:T(1024)}, f32[768]{0:T(1024)S(1)}, u32[]{:S(2)}) copy-start(f32[768]{0:T(1024)S(1)} %get-tuple-element.1912) | copy-start | bytes 9220
  22.0 33.1 %copy-start.137 = (f32[768]{0:T(1024)}, f32[768]{0:T(1024)S(1)}, u32[]{:S(2)}) copy-start(f32[768]{0:T(1024)S(1)} %get-tuple-element.1913) | copy-start | bytes 9220
  22.0 33.1 %copy-start.139 = (f32[768]{0:T(1024)}, f32[768]{0:T(1024)S(1)}, u32[]{:S(2)}) copy-start(f32[768]{0:T(1024)S(1)} %get-tuple-element.1914) | copy-start | bytes 9220
  22.0 33.1 %copy-start.141 = (f32[768]{0:T(1024)}, f32[768]{0:T(1024)S(1)}, u32[]{:S(2)}) copy-start(f32[768]{0:T(1024)S(1)} %get-tuple-element.2178) | copy-start | bytes 9220
  22.0 33.1 %copy-start.143 = (f32[768]{0:T(1024)}, f32[768]{0:T(1024)S(1)}, u32[]{:S(2)}) copy-start(f32[768]{0:T(1024)S(1)} %get-tuple-element.2179) | copy-start | bytes 9220
  22.0 33.1 %copy-start.145 = (f32[768]{0:T(1024)}, f32[768]{0:T(1024)S(1)}, u32[]{:S(2)}) copy-start(f32[768]{0:T(1024)S(1)} %get-tuple-element.2180) | copy-start | bytes 9220
  33.8 23.1 %copy-start.31 = (f32[128,768]{1,0:T(8,128)}, f32[128,768]{1,0:T(8,128)S(1)}, u32[]{:S(2)}) copy-start(f32[128,768]{1,0:T(8,128)S(1)} %fusion.335) | copy-start | bytes 1179652
  58.2 6.3 copy-start.67
  97.2 36.8 %copy-start.50 = (f32[1,6,64]{2,1,0:T(8,128)}, f32[1,6,64]{2,1,0:T(8,128)S(1)}, u32[]{:S(2)}) copy-start(f32[1,6,64]{2,1,0:T(8,128)S(1)} %reduce_window_sum.42) | copy-start | bytes 4612 | tf_op jit(solution)/shard_map/while
  147.8 36.8 %copy-start.50 = (f32[1,6,64]{2,1,0:T(8,128)}, f32[1,6,64]{2,1,0:T(8,128)S(1)}, u32[]{:S(2)}) copy-start(f32[1,6,64]{2,1,0:T(8,128)S(1)} %reduce_window_sum.42) | copy-start | bytes 4612 | tf_op jit(solution)/shard_map/while
  204.1 34.5 %copy-start.6 = (f32[1,6,64]{2,1,0:T(8,128)}, f32[1,6,64]{2,1,0:T(8,128)S(1)}, u32[]{:S(2)}) copy-start(f32[1,6,64]{2,1,0:T(8,128)S(1)} %reduce_window_sum.43) | copy-start | bytes 4612 | tf_op jit(solution)/shard_map/jvp()/while
  205.4 34.5 %copy-start.77 = (f32[6,64]{1,0:T(8,128)}, f32[6,64]{1,0:T(8,128)S(1)}, u32[]{:S(2)}) copy-start(f32[6,64]{1,0:T(8,128)S(1)} %get-tuple-element.2729) | copy-start | bytes 4612 | tf_op jit(solution)/shard_map/jvp()/while
  261.9 34.6 %copy-start.6 = (f32[1,6,64]{2,1,0:T(8,128)}, f32[1,6,64]{2,1,0:T(8,128)S(1)}, u32[]{:S(2)}) copy-start(f32[1,6,64]{2,1,0:T(8,128)S(1)} %reduce_window_sum.43) | copy-start | bytes 4612 | tf_op jit(solution)/shard_map/jvp()/while
  263.2 34.5 %copy-start.77 = (f32[6,64]{1,0:T(8,128)}, f32[6,64]{1,0:T(8,128)S(1)}, u32[]{:S(2)}) copy-start(f32[6,64]{1,0:T(8,128)S(1)} %get-tuple-element.2729) | copy-start | bytes 4612 | tf_op jit(solution)/shard_map/jvp()/while
  334.2 28.6 %copy-start.22 = (f32[128,1024]{1,0:T(8,128)}, f32[128,1024]{1,0:T(8,128)S(1)}, u32[]{:S(2)}) copy-start(f32[128,1024]{1,0:T(8,128)S(1)} %get-tuple-element.2173) | copy-start | bytes 1572868
  334.2 28.6 %copy-start.179 = (f32[128]{0:T(128)}, f32[128]{0:T(128)S(1)}, u32[]{:S(2)}) copy-start(f32[128]{0:T(128)S(1)} %fusion.319) | copy-start | bytes 1540
  334.2 244.0 %all-gather.44.cloned.1.call-start = ((), (), s32[]{:S(2)}) async-start(), calls=%async_computation.23 | async-start | bytes 1310720 | tf_op jit(solution)/shard_map/all_gather | solution.py:248
  357.1 6.4 copy-start.86
  379.5 202.1 %all-gather.56.cloned.1.call-start = ((), (), s32[]{:S(2)}) async-start(), calls=%async_computation.33 | async-start | bytes 1966080 | tf_op jit(solution)/shard_map/all_gather | solution.py:246
  422.1 9.5 copy-start.1
  425.8 5.8 copy-start.37
  425.8 5.8 copy-start.74
  490.5 9.5 copy-start.1
  494.2 5.8 copy-start.37
  527.0 58.3 %all-gather.40.cloned.1.call-start = ((), (), s32[]{:S(2)}) async-start(), calls=%async_computation.20 | async-start | bytes 1966080 | tf_op jit(solution)/shard_map/all_gather | solution.py:247
  527.7 61.5 %all-gather.46.cloned.1.call-start = ((), (), s32[]{:S(2)}) async-start(), calls=%async_computation.25 | async-start | bytes 1310720 | tf_op jit(solution)/shard_map/all_gather | solution.py:242
  528.3 89.3 %all-gather.48.cloned.1.call-start = ((), (), s32[]{:S(2)}) async-start(), calls=%async_computation.26 | async-start | bytes 3604480 | tf_op jit(solution)/shard_map/all_gather | solution.py:249
  528.9 117.2 %all-gather.50.cloned.1.call-start = ((), (), s32[]{:S(2)}) async-start(), calls=%async_computation.28 | async-start | bytes 3604480 | tf_op jit(solution)/shard_map/all_gather | solution.py:250
  529.5 134.8 %all-gather.54.cloned.1.call-start = ((), (), s32[]{:S(2)}) async-start(), calls=%async_computation.31 | async-start | bytes 1310720 | tf_op jit(solution)/shard_map/all_gather | solution.py:251
  530.0 162.7 %all-gather.52.cloned.1.call-start = ((), (), s32[]{:S(2)}) async-start(), calls=%async_computation.30 | async-start | bytes 3604480 | tf_op jit(solution)/shard_map/all_gather | solution.py:243
  536.6 6.1 copy-start.26
  539.2 291.3 %all-reduce.40.cloned.1.call-start = ((), (), s32[]{:S(2)}) async-start(), calls=%async_computation.34 | async-start | bytes 249856 | tf_op jit(solution)/shard_map/psum | solution.py:280
  564.7 332.1 %reduce-scatter.11.cloned.1.call-start = ((), (), s32[]{:S(2)}) async-start(), calls=%async_computation.18 | async-start | bytes 884736 | tf_op jit(solution)/shard_map/reduce_scatter | solution.py:271
  567.1 395.9 %reduce-scatter.9.cloned.1.call-start = ((), (), s32[]{:S(2)}) async-start(), calls=%async_computation.17 | async-start | bytes 884736 | tf_op jit(solution)/shard_map/reduce_scatter | solution.py:270
  578.2 454.4 %reduce-scatter.17.cloned.1.call-start = ((), (), s32[]{:S(2)}) async-start(), calls=%async_computation.24 | async-start | bytes 1769472 | tf_op jit(solution)/shard_map/reduce_scatter | solution.py:274
  581.5 519.6 %reduce-scatter.13.cloned.1.call-start = ((), (), s32[]{:S(2)}) async-start(), calls=%async_computation.19 | async-start | bytes 1769472 | tf_op jit(solution)/shard_map/reduce_scatter | solution.py:272
  584.9 584.7 %reduce-scatter.15.cloned.1.call-start = ((), (), s32[]{:S(2)}) async-start(), calls=%async_computation.21 | async-start | bytes 1769472 | tf_op jit(solution)/shard_map/reduce_scatter | solution.py:273
  588.6 656.3 %reduce-scatter.19.cloned.1.call-start = ((), (), s32[]{:S(2)}) async-start(), calls=%async_computation.27 | async-start | bytes 3244032 | tf_op jit(solution)/shard_map/reduce_scatter | solution.py:275
  622.4 698.0 %reduce-scatter.21.cloned.1.call-start = ((), (), s32[]{:S(2)}) async-start(), calls=%async_computation.29 | async-start | bytes 3244032 | tf_op jit(solution)/shard_map/reduce_scatter | solution.py:276
  651.0 745.5 %reduce-scatter.23.cloned.1.call-start = ((), (), s32[]{:S(2)}) async-start(), calls=%async_computation.32 | async-start | bytes 3244032 | tf_op jit(solution)/shard_map/reduce_scatter | solution.py:277
  (248 other events, 617.7 us)
Sparse Core Ops, SparseCore 0:
  9.6 22.3 all-gather.25
  33.5 19.7 all-gather.21
  54.9 28.4 all-gather.23
  84.8 28.6 all-gather.27
  114.9 28.5 all-gather.29
  144.9 43.4 all-gather.31
  190.0 43.4 all-gather.33
  235.1 43.8 all-gather.35
  281.1 17.0 all-gather.37
  334.4 19.6 all-gather.41
  379.7 16.7 all-gather.43
  527.1 19.5 all-gather.55
  548.2 22.1 all-gather.39
  572.4 16.7 all-gather.45
  590.6 27.0 all-gather.47
  619.0 27.0 all-gather.49
  647.5 16.6 all-gather.53
  665.7 27.0 all-gather.51
  700.9 129.5 all-reduce.39
  834.2 62.4 reduce-scatter.10
  900.6 62.2 reduce-scatter.8
  967.0 65.5 reduce-scatter.16
  1036.6 64.5 reduce-scatter.12
  1105.0 64.5 reduce-scatter.14
  1173.7 71.2 reduce-scatter.18
  1248.9 71.4 reduce-scatter.20
  1324.4 72.0 reduce-scatter.22
where the time goes:
time: 1420 us
  waiting for transfers between devices  841 us (59%)
  other arithmetic  256 us (18%)
  matrix products  169 us (12%)
  local copies, waits for them, and re-layouts  109 us (8%)
  blocking collectives  20.5 us (1%)
  between operations  16.6 us (1%)
    another operation x28, other arithmetic, span_step(): jax.scipy.linalg.solve_triangular(system, rhs, lower=True, unit_diagonal=...  185 us
    psum x1, waiting for transfers between devices, body(): lax.psum((small_terms[0], small_terms[1], small_terms[2], small_terms[3],...  127 us
    reduce_scatter x1, waiting for transfers between devices, body(): lax.psum_scatter(own_rows[7], 'rep', scatter_dimension=1, tiled=True)  76 us
    reduce_scatter x1, waiting for transfers between devices, body(): lax.psum_scatter(own_rows[6], 'rep', scatter_dimension=1, tiled=True)  75.5 us
    reduce_scatter x1, waiting for transfers between devices, body(): lax.psum_scatter(own_rows[5], 'rep', scatter_dimension=1, tiled=True)  75.4 us
    reduce_scatter x1, waiting for transfers between devices, body(): lax.psum_scatter(own_rows[4], 'rep', scatter_dimension=1, tiled=True)  69.6 us
    reduce_scatter x1, waiting for transfers between devices, body(): lax.psum_scatter(own_rows[2], 'rep', scatter_dimension=1, tiled=True)  68.6 us
    reduce_scatter x1, waiting for transfers between devices, body(): lax.psum_scatter(own_rows[3], 'rep', scatter_dimension=1, tiled=True)  68.4 us
  transfers between devices with their start and end apart: 27, of which 17 were waited for; matrix products, arithmetic and copies ran while one was open for 35% of the time, Pallas kernels for 0%

commit v1 on v0

--- a/solution.py
+++ b/solution.py
@@ -278,19 +278,22 @@
     )
     small_terms = (mix_small[0], g_gain_mid) + tuple(mix_small[1:])
     small_final = lax.psum(
-        (
-            small_terms[0],
-            small_terms[1],
-            small_terms[2],
-            small_terms[3],
-            small_terms[4],
-            small_terms[5],
-            small_terms[6],
-            small_terms[7],
-            small_terms[8],
-            small_terms[9],
+        lax.psum(
+            (
+                small_terms[0],
+                small_terms[1],
+                small_terms[2],
+                small_terms[3],
+                small_terms[4],
+                small_terms[5],
+                small_terms[6],
+                small_terms[7],
+                small_terms[8],
+                small_terms[9],
+            ),
+            "rep",
         ),
-        ("shard", "rep"),
+        "shard",
     )
     g_query, g_key, g_value, g_gate_out, g_out, g_ffgate, g_ffup, g_down = large_final
     (

time: 1420 us -> 1470 us (1.035)
  waiting for transfers between devices: 841 us -> 899 us
    psum x1, waiting for transfers between devices: 127 us -> 57.6 us  [body(): lax.psum((small_terms[0], small_terms[1], small_terms[2], small_terms[3],...]
    psum x0 -> x1, waiting for transfers between devices: none -> 24.8 us  [body(): lax.psum(lax.psum((small_terms[0], small_terms[1], small_terms[2], small_...]
    all_gather x1, waiting for transfers between devices: 0.02 us -> 18.7 us  [body(): lax.all_gather(mix_pairs[0][0], 'shard', axis=0, tiled=True)]
    all_gather x1, waiting for transfers between devices: 0.02 us -> 18.7 us  [body(): lax.all_gather(mix_pairs[4][1], 'shard', axis=0, tiled=True)]
    all_gather x1, waiting for transfers between devices: 0.02 us -> 18 us  [body(): lax.all_gather(mix_pairs[2][1], 'shard', axis=0, tiled=True)]
    all_gather x1, waiting for transfers between devices: 0.02 us -> 17.4 us  [body(): lax.all_gather(mix_pairs[3][1], 'shard', axis=0, tiled=True)]
    all_gather x1, waiting for transfers between devices: 0.51 us -> 15.3 us  [body(): lax.all_gather(ffn_pairs[0][0], 'shard', axis=0, tiled=True)]
  transfers between devices with their start and end apart: 27 -> 28, of which waited for: 17 -> 23; matrix products, arithmetic and copies ran while one was open for 35% -> 20% of each run, Pallas kernels for 0% -> 0%
where the time goes in v1:
time: 1470 us; the launch traced here: 1460 us
  waiting for transfers between devices  899 us (61%)
  other arithmetic  255 us (17%)
  matrix products  160 us (11%)
  local copies, waits for them, and re-layouts  110 us (7%)
  blocking collectives  17.2 us (1%)
  between operations  16.6 us (1%)
    another operation x28, other arithmetic, span_step(): jax.scipy.linalg.solve_triangular(system, rhs, lower=True, unit_diagonal=...  185 us
    reduce_scatter x1, waiting for transfers between devices, body(): lax.psum_scatter(own_rows[7], 'rep', scatter_dimension=1, tiled=True)  76.4 us
    reduce_scatter x1, waiting for transfers between devices, body(): lax.psum_scatter(own_rows[6], 'rep', scatter_dimension=1, tiled=True)  75.8 us
    reduce_scatter x1, waiting for transfers between devices, body(): lax.psum_scatter(own_rows[5], 'rep', scatter_dimension=1, tiled=True)  75.3 us
    reduce_scatter x1, waiting for transfers between devices, body(): lax.psum_scatter(own_rows[4], 'rep', scatter_dimension=1, tiled=True)  69.6 us
    reduce_scatter x1, waiting for transfers between devices, body(): lax.psum_scatter(own_rows[3], 'rep', scatter_dimension=1, tiled=True)  68.4 us
    reduce_scatter x1, waiting for transfers between devices, body(): lax.psum_scatter(own_rows[2], 'rep', scatter_dimension=1, tiled=True)  68.3 us
    reduce_scatter x1, waiting for transfers between devices, body(): lax.psum_scatter(own_rows[1], 'rep', scatter_dimension=1, tiled=True)  67.2 us
  transfers between devices with their start and end apart: 28, of which 23 were waited for; matrix products, arithmetic and copies ran while one was open for 20% of the time, Pallas kernels for 0%

profile of v1, /device:TPU:0, one launch (start us, length us, event | category | flops | bytes accessed | tf_op | source)
XLA Modules:
  0.0 1462.9 jit_solution(793152101740696060)
XLA Ops:
  20.0 12.0 all-gather.26.cloned.1.call-done
  33.8 19.4 %all-gather.22.cloned.1.call-done = bf16[1024,768]{1,0:T(8,128)(2,1)} async-done(((bf16[256,768]{1,0:T(8,128)(2,1)}), bf16[1024,768]{1,0:T(8,128)(2,1)}) %all-gather.22.cloned.1.call-update) | async-done | bytes 1572880 | tf_op jit(solution)/shard_map/all_gather | solution.py:228
  66.9 16.4 %all-gather.24.cloned.1.call-done = bf16[1024,1536]{1,0:T(8,128)(2,1)} async-done(((bf16[256,1536]{1,0:T(8,128)(2,1)}), bf16[1024,1536]{1,0:T(8,128)(2,1)}) %all-gather.24.cloned.1.call-update) | async-done | bytes 3145744 | tf_op jit(solution)/shard_map/all_gather | solution.py:229
  83.3 2.5 fusion.334
  87.7 2.3 reshape_reshape.12
  90.0 2.4 copy.216
  98.2 119.6 %while.104 = (s32[]{:T(128)}, f32[1,6,128,256]{3,2,1,0:T(8,128)S(1)}, f32[2,1,6,64,256]{4,3,2,1,0:T(8,128)}, f32[2,1,6,64,64]{4,3,2,1,0:T(8,128)}, f32[2,1,6,64,...) while((s32[]{:T(128)}, ...), condition=%wide.region_11.13_spmd.clone.clone, body=%wide.region_9.12_spmd.clone.clone.sunk | while | flops 719999424 | bytes 38057020 | solution.py:84
  106.5 30.2 %custom-call.46 = f32[6,1,64,64]{2,3,1,0:T(8,128)S(1)} custom-call(f32[6,1,64,64]{3,2,1,0:T(8,128)} %add_bitcast_fusion.5), custom_call_target="InvertDiagBlocksLowerTriangular" | custom-call | tf_op jit(solution)/shard_map/jvp()/while/body/eval_jaxpr/jit(_solve_triangular)/vmap()/triangular_solve/custom-call.1 | solution.py:70
  139.7 2.5 bitcast_dynamic-update-slice_fusion.19
  142.3 2.3 bitcast_dynamic-update-slice_fusion.21
  166.1 30.2 %custom-call.46 = f32[6,1,64,64]{2,3,1,0:T(8,128)S(1)} custom-call(f32[6,1,64,64]{3,2,1,0:T(8,128)} %add_bitcast_fusion.5), custom_call_target="InvertDiagBlocksLowerTriangular" | custom-call | tf_op jit(solution)/shard_map/jvp()/while/body/eval_jaxpr/jit(_solve_triangular)/vmap()/triangular_solve/custom-call.1 | solution.py:70
  199.4 2.7 bitcast_dynamic-update-slice_fusion.19
  202.1 2.3 bitcast_dynamic-update-slice_fusion.21
  217.8 2.7 copy.226
  222.2 83.6 %while.103 = (s32[]{:T(128)}, f32[1,6,128,256]{3,2,1,0:T(8,128)S(1)}, f32[2,1,6,64,256]{4,3,2,1,0:T(8,128)}, f32[2,1,6,64]{3,2,1,0:T(8,128)}, s32[2,1,64]{2,1,0:...) while((s32[]{:T(128)}, ...), condition=%wide.region_5.7_spmd.clone.clone, body=%wide.region_3.6_spmd.clone.clone.sunk | while | flops 719243328 | bytes 16518565 | solution.py:84
  227.8 29.5 %custom-call.45 = f32[6,1,64,64]{2,3,1,0:T(8,128)S(1)} custom-call(f32[6,1,64,64]{3,2,1,0:T(8,128)S(1)} %fusion.510), custom_call_target="InvertDiagBlocksLowerTriangular" | custom-call | tf_op jit(solution)/shard_map/while/body/eval_jaxpr/jit(_solve_triangular)/vmap()/triangular_solve/custom-call.1 | solution.py:70
  269.3 29.5 %custom-call.45 = f32[6,1,64,64]{2,3,1,0:T(8,128)S(1)} custom-call(f32[6,1,64,64]{3,2,1,0:T(8,128)S(1)} %fusion.510), custom_call_target="InvertDiagBlocksLowerTriangular" | custom-call | tf_op jit(solution)/shard_map/while/body/eval_jaxpr/jit(_solve_triangular)/vmap()/triangular_solve/custom-call.1 | solution.py:70
  312.7 3.8 multiply_convert_fusion.3
  317.9 2.7 multiply_reduce_fusion.8
  320.8 4.8 fusion.336
  325.6 4.7 fusion.337
  330.3 7.2 multiply_convert_fusion
  337.5 5.6 fusion.338
  343.1 5.7 multiply_reduce_fusion.6
  350.4 5.0 fusion.243
  355.4 2.4 reshape_reshape.13
  357.9 2.7 fusion.234
  369.3 133.1 %while.102 = (s32[]{:T(128)}, f32[1,6,128,256]{2,3,1,0:T(8,128)S(1)}, f32[2,1,6,64,128]{4,3,2,1,0:T(8,128)}, f32[2,1,6,64,128]{4,3,0,2,1:T(8,128)}, f32[2,1,6,64...) while((s32[]{:T(128)}, ...), condition=%wide.region_24.26_spmd.clone, body=%wide.region_14.25_spmd.clone.sunk | while | flops 1457530112 | bytes 73533384 | solution.py:84
  375.4 30.9 %custom-call.44 = f32[6,1,64,64]{2,3,1,0:T(8,128)} custom-call(f32[6,1,64,64]{3,2,1,0:T(8,128)} %add_bitcast_fusion.4), custom_call_target="InvertDiagBlocksLowerTriangular" | custom-call | tf_op jit(solution)/shard_map/transpose(jvp())/while/body/eval_jaxpr/jit(_solve_triangular)/vmap()/triangular_solve | solution.py:70
  408.1 2.6 fusion.487
  441.8 30.9 %custom-call.44 = f32[6,1,64,64]{2,3,1,0:T(8,128)} custom-call(f32[6,1,64,64]{3,2,1,0:T(8,128)} %add_bitcast_fusion.4), custom_call_target="InvertDiagBlocksLowerTriangular" | custom-call | tf_op jit(solution)/shard_map/transpose(jvp())/while/body/eval_jaxpr/jit(_solve_triangular)/vmap()/triangular_solve | solution.py:70
  474.4 2.6 fusion.487
  520.1 2.6 multiply_reduce_fusion.16
  537.5 3.1 fusion.225
  550.4 8.6 all-gather.1
  559.0 57.6 %all-reduce.42.cloned.1.call-done = (f32[1024]{0:T(1024)}, f32[4,768]{1,0:T(4,128)}, f32[4,768]{1,0:T(4,128)}, f32[4,1536]{1,0:T(4,128)}, f32[1024,6]{0,1:T(8,12...) async-done(((f32[1024]{0:T(1024)}, f32[4,768]{1,0:T(4,128)}, f32[4,768]{1,0:T(4,128)}, f32[4,1536]{1,0:T(4,128)}, ...) | async-done | bytes 107584 | tf_op jit(solution)/shard_map/psum | solution.py:281
  616.6 18.7 %all-gather.38.cloned.1.call-done = bf16[512,1024]{1,0:T(8,128)(2,1)} async-done(((bf16[128,1024]{1,0:T(8,128)(2,1)}), bf16[512,1024]{1,0:T(8,128)(2,1)}) %all-gather.38.cloned.1.call-update) | async-done | bytes 1048592 | tf_op jit(solution)/shard_map/all_gather | solution.py:240
  635.3 2.4 fusion.244
  637.8 8.6 all-gather
  647.8 8.8 all-gather.42.cloned.1.call-done
  656.6 18.7 %all-gather.44.cloned.1.call-done = bf16[512,1024]{1,0:T(8,128)(2,1)} async-done(((bf16[128,1024]{1,0:T(8,128)(2,1)}), bf16[512,1024]{1,0:T(8,128)(2,1)}) %all-gather.44.cloned.1.call-update) | async-done | bytes 1048592 | tf_op jit(solution)/shard_map/all_gather | solution.py:248
  675.3 3.1 fusion.280
  678.5 18.0 %all-gather.56.cloned.1.call-done = bf16[1,512,1536]{2,1,0:T(8,128)(2,1)} async-done(((bf16[1,128,1536]{2,1,0:T(8,128)(2,1)}), bf16[1,512,1536]{2,1,0:T(8,128)(2,1)}) %all-gather.56.cloned.1.call-update) | async-done | bytes 1572880 | tf_op jit(solution)/shard_map/all_gather | solution.py:246
  696.5 3.3 fusion.223
  700.2 17.4 %all-gather.40.cloned.1.call-done = bf16[512,1536]{1,0:T(8,128)(2,1)} async-done(((bf16[128,1536]{1,0:T(8,128)(2,1)}), bf16[512,1536]{1,0:T(8,128)(2,1)}) %all-gather.40.cloned.1.call-update) | async-done | bytes 1572880 | tf_op jit(solution)/shard_map/all_gather | solution.py:247
  717.6 3.3 fusion.291
  721.0 15.3 %all-gather.46.cloned.1.call-done = bf16[512,1024]{1,0:T(8,128)(2,1)} async-done(((bf16[128,1024]{1,0:T(8,128)(2,1)}), bf16[512,1024]{1,0:T(8,128)(2,1)}) %all-gather.46.cloned.1.call-update) | async-done | bytes 1048592 | tf_op jit(solution)/shard_map/all_gather | solution.py:242
  736.3 28.5 %all-gather.48.cloned.1.call-done = bf16[512,2816]{1,0:T(8,128)(2,1)} async-done(((bf16[128,2816]{1,0:T(8,128)(2,1)}), bf16[512,2816]{1,0:T(8,128)(2,1)}) %all-gather.48.cloned.1.call-update) | async-done | bytes 2883600 | tf_op jit(solution)/shard_map/all_gather | solution.py:249
  764.8 4.7 fusion.286
  769.6 23.7 %all-gather.50.cloned.1.call-done = bf16[512,2816]{1,0:T(8,128)(2,1)} async-done(((bf16[128,2816]{1,0:T(8,128)(2,1)}), bf16[512,2816]{1,0:T(8,128)(2,1)}) %all-gather.50.cloned.1.call-update) | async-done | bytes 2883600 | tf_op jit(solution)/shard_map/all_gather | solution.py:250
  793.2 4.7 fusion.284
  798.1 13.3 all-gather.54.cloned.1.call-done
  811.4 28.6 %all-gather.52.cloned.1.call-done = bf16[512,2816]{1,0:T(8,128)(2,1)} async-done(((bf16[128,2816]{1,0:T(8,128)(2,1)}), bf16[512,2816]{1,0:T(8,128)(2,1)}) %all-gather.52.cloned.1.call-update) | async-done | bytes 2883600 | tf_op jit(solution)/shard_map/all_gather | solution.py:243
  840.0 4.4 fusion.250
  846.7 4.3 fusion.226
  851.0 24.8 %all-reduce.44.cloned.1.call-done = (f32[1024]{0:T(1024)}, f32[4,768]{1,0:T(4,128)}, f32[4,768]{1,0:T(4,128)}, f32[4,1536]{1,0:T(4,128)}, f32[1024,6]{0,1:T(8,12...) async-done(((f32[1024]{0:T(1024)}, f32[4,768]{1,0:T(4,128)}, f32[4,768]{1,0:T(4,128)}, f32[4,1536]{1,0:T(4,128)}, ...) | async-done | bytes 107584 | tf_op jit(solution)/shard_map/psum | solution.py:280
  875.8 67.2 %reduce-scatter.11.cloned.1.call-done = f32[256,96]{0,1:T(8,128)} async-done(((f32[256,768]{0,1:T(8,128)}), f32[256,96]{0,1:T(8,128)}) %reduce-scatter.11.cloned.1.call-update) | async-done | bytes 98320 | tf_op jit(solution)/shard_map/reduce_scatter | solution.py:271
  943.0 66.2 %reduce-scatter.9.cloned.1.call-done = f32[256,96]{0,1:T(8,128)} async-done(((f32[256,768]{0,1:T(8,128)}), f32[256,96]{0,1:T(8,128)}) %reduce-scatter.9.cloned.1.call-update) | async-done | bytes 98320 | tf_op jit(solution)/shard_map/reduce_scatter | solution.py:270
  1009.2 69.6 %reduce-scatter.17.cloned.1.call-done = f32[384,128]{1,0:T(8,128)} async-done(((f32[384,1024]{1,0:T(8,128)}), f32[384,128]{1,0:T(8,128)}) %reduce-scatter.17.cloned.1.call-update) | async-done | bytes 196624 | tf_op jit(solution)/shard_map/reduce_scatter | solution.py:274
  1078.8 68.3 %reduce-scatter.13.cloned.1.call-done = f32[256,192]{0,1:T(8,128)} async-done(((f32[256,1536]{0,1:T(8,128)}), f32[256,192]{0,1:T(8,128)}) %reduce-scatter.13.cloned.1.call-update) | async-done | bytes 196624 | tf_op jit(solution)/shard_map/reduce_scatter | solution.py:272
  1147.2 68.4 %reduce-scatter.15.cloned.1.call-done = f32[256,192]{0,1:T(8,128)} async-done(((f32[256,1536]{0,1:T(8,128)}), f32[256,192]{0,1:T(8,128)}) %reduce-scatter.15.cloned.1.call-update) | async-done | bytes 196624 | tf_op jit(solution)/shard_map/reduce_scatter | solution.py:273
  1215.5 75.3 %reduce-scatter.19.cloned.1.call-done = f32[256,352]{0,1:T(8,128)} async-done(((f32[256,2816]{0,1:T(8,128)}), f32[256,352]{0,1:T(8,128)}) %reduce-scatter.19.cloned.1.call-update) | async-done | bytes 360464 | tf_op jit(solution)/shard_map/reduce_scatter | solution.py:275
  1290.8 75.8 %reduce-scatter.21.cloned.1.call-done = f32[256,352]{0,1:T(8,128)} async-done(((f32[256,2816]{0,1:T(8,128)}), f32[256,352]{0,1:T(8,128)}) %reduce-scatter.21.cloned.1.call-update) | async-done | bytes 360464 | tf_op jit(solution)/shard_map/reduce_scatter | solution.py:276
  1366.6 76.4 %reduce-scatter.23.cloned.1.call-done = f32[704,128]{1,0:T(8,128)} async-done(((f32[704,1024]{1,0:T(8,128)}), f32[704,128]{1,0:T(8,128)}) %reduce-scatter.23.cloned.1.call-update) | async-done | bytes 360464 | tf_op jit(solution)/shard_map/reduce_scatter | solution.py:277
  (1001 shorter events, 250.3 us)
Async XLA Ops:
  7.2 7.9 copy-start
  7.2 24.8 %all-gather.26.cloned.1.call-start = ((), (), s32[]{:S(2)}) async-start(), calls=%async_computation.10 | async-start | bytes 1966080 | tf_op jit(solution)/shard_map/all_gather | solution.py:227
  7.9 45.2 %all-gather.22.cloned.1.call-start = ((), (), s32[]{:S(2)}) async-start(), calls=%async_computation.8 | async-start | bytes 1966080 | tf_op jit(solution)/shard_map/all_gather | solution.py:228
  8.7 74.6 %all-gather.24.cloned.1.call-start = ((), (), s32[]{:S(2)}) async-start(), calls=%async_computation.9 | async-start | bytes 3932160 | tf_op jit(solution)/shard_map/all_gather | solution.py:229
  9.4 303.2 %all-gather.28.cloned.1.call-start = ((), (), s32[]{:S(2)}) async-start(), calls=%async_computation.11 | async-start | bytes 3932160 | tf_op jit(solution)/shard_map/all_gather | solution.py:230
  10.0 307.9 %all-gather.30.cloned.1.call-start = ((), (), s32[]{:S(2)}) async-start(), calls=%async_computation.12 | async-start | bytes 3932160 | tf_op jit(solution)/shard_map/all_gather | solution.py:231
  10.6 310.2 %all-gather.32.cloned.1.call-start = ((), (), s32[]{:S(2)}) async-start(), calls=%async_computation.13 | async-start | bytes 7208960 | tf_op jit(solution)/shard_map/all_gather | solution.py:232
  11.2 314.3 %all-gather.34.cloned.1.call-start = ((), (), s32[]{:S(2)}) async-start(), calls=%async_computation.14 | async-start | bytes 7208960 | tf_op jit(solution)/shard_map/all_gather | solution.py:233
  12.0 5.9 copy-start.186
  12.0 7.2 copy-start.176
  12.0 7.2 copy-start.177
  12.0 318.2 %all-gather.36.cloned.1.call-start = ((), (), s32[]{:S(2)}) async-start(), calls=%async_computation.15 | async-start | bytes 7208960 | tf_op jit(solution)/shard_map/all_gather | solution.py:234
  12.8 603.8 %all-reduce.42.cloned.1.call-start = ((), (), s32[]{:S(2)}) async-start(), calls=%async_computation.34 | async-start | bytes 249856 | tf_op jit(solution)/shard_map/psum | solution.py:281
  13.9 71.9 %copy-start.159 = (f32[128]{0:T(128)}, f32[128]{0:T(128)S(1)}, u32[]{:S(2)}) copy-start(f32[128]{0:T(128)S(1)} %get-tuple-element.2175) | copy-start | bytes 1540
  13.9 71.9 %copy-start.162 = (f32[128]{0:T(128)}, f32[128]{0:T(128)S(1)}, u32[]{:S(2)}) copy-start(f32[128]{0:T(128)S(1)} %get-tuple-element.2176) | copy-start | bytes 1540
  13.9 71.9 %copy-start.165 = (f32[128]{0:T(128)}, f32[128]{0:T(128)S(1)}, u32[]{:S(2)}) copy-start(f32[128]{0:T(128)S(1)} %get-tuple-element.2177) | copy-start | bytes 1540
  14.0 71.8 %copy-start.110 = (f32[1536]{0:T(1024)}, f32[1536]{0:T(1024)S(1)}, u32[]{:S(2)}) copy-start(f32[1536]{0:T(1024)S(1)} %get-tuple-element.1907) | copy-start | bytes 18436
  14.0 71.8 %copy-start.112 = (f32[1536]{0:T(1024)}, f32[1536]{0:T(1024)S(1)}, u32[]{:S(2)}) copy-start(f32[1536]{0:T(1024)S(1)} %get-tuple-element.1908) | copy-start | bytes 18436
  14.1 71.8 %copy-start.114 = (f32[1536]{0:T(1024)}, f32[1536]{0:T(1024)S(1)}, u32[]{:S(2)}) copy-start(f32[1536]{0:T(1024)S(1)} %get-tuple-element.1909) | copy-start | bytes 18436
  14.1 71.8 %copy-start.116 = (f32[1536]{0:T(1024)}, f32[1536]{0:T(1024)S(1)}, u32[]{:S(2)}) copy-start(f32[1536]{0:T(1024)S(1)} %get-tuple-element.1910) | copy-start | bytes 18436
  14.2 69.1 %copy-start.27 = (bf16[128,1024]{1,0:T(8,128)(2,1)}, bf16[128,1024]{1,0:T(8,128)(2,1)S(1)}, u32[]{:S(2)}) copy-start(bf16[128,1024]{1,0:T(8,128)(2,1)S(1)} %fusion.255) | copy-start | bytes 786436
  19.3 35.7 %copy-start.135 = (f32[768]{0:T(1024)}, f32[768]{0:T(1024)S(1)}, u32[]{:S(2)}) copy-start(f32[768]{0:T(1024)S(1)} %get-tuple-element.1911) | copy-start | bytes 9220
  19.3 35.7 %copy-start.137 = (f32[768]{0:T(1024)}, f32[768]{0:T(1024)S(1)}, u32[]{:S(2)}) copy-start(f32[768]{0:T(1024)S(1)} %get-tuple-element.2191) | copy-start | bytes 9220
  19.3 35.7 %copy-start.138 = (f32[768]{0:T(1024)}, f32[768]{0:T(1024)S(1)}, u32[]{:S(2)}) copy-start(f32[768]{0:T(1024)S(1)} %get-tuple-element.1912) | copy-start | bytes 9220
  19.3 35.7 %copy-start.140 = (f32[768]{0:T(1024)}, f32[768]{0:T(1024)S(1)}, u32[]{:S(2)}) copy-start(f32[768]{0:T(1024)S(1)} %get-tuple-element.1913) | copy-start | bytes 9220
  19.3 35.7 %copy-start.142 = (f32[768]{0:T(1024)}, f32[768]{0:T(1024)S(1)}, u32[]{:S(2)}) copy-start(f32[768]{0:T(1024)S(1)} %get-tuple-element.1914) | copy-start | bytes 9220
  19.3 35.7 %copy-start.144 = (f32[768]{0:T(1024)}, f32[768]{0:T(1024)S(1)}, u32[]{:S(2)}) copy-start(f32[768]{0:T(1024)S(1)} %get-tuple-element.2188) | copy-start | bytes 9220
  19.3 35.7 %copy-start.146 = (f32[768]{0:T(1024)}, f32[768]{0:T(1024)S(1)}, u32[]{:S(2)}) copy-start(f32[768]{0:T(1024)S(1)} %get-tuple-element.2189) | copy-start | bytes 9220
  19.4 35.7 %copy-start.148 = (f32[768]{0:T(1024)}, f32[768]{0:T(1024)S(1)}, u32[]{:S(2)}) copy-start(f32[768]{0:T(1024)S(1)} %get-tuple-element.2190) | copy-start | bytes 9220
  33.8 23.1 %copy-start.35 = (f32[128,768]{1,0:T(8,128)}, f32[128,768]{1,0:T(8,128)S(1)}, u32[]{:S(2)}) copy-start(f32[128,768]{1,0:T(8,128)S(1)} %fusion.335) | copy-start | bytes 1179652
  58.0 6.0 copy-start.70
  101.8 37.9 %copy-start.8 = (f32[1,6,64]{2,1,0:T(8,128)}, f32[1,6,64]{2,1,0:T(8,128)S(1)}, u32[]{:S(2)}) copy-start(f32[1,6,64]{2,1,0:T(8,128)S(1)} %reduce_window_sum.43) | copy-start | bytes 4612 | tf_op jit(solution)/shard_map/jvp()/while
  103.1 36.6 %copy-start.80 = (f32[6,64]{1,0:T(8,128)}, f32[6,64]{1,0:T(8,128)S(1)}, u32[]{:S(2)}) copy-start(f32[6,64]{1,0:T(8,128)S(1)} %get-tuple-element.2739) | copy-start | bytes 4612 | tf_op jit(solution)/shard_map/jvp()/while
  161.4 38.0 %copy-start.8 = (f32[1,6,64]{2,1,0:T(8,128)}, f32[1,6,64]{2,1,0:T(8,128)S(1)}, u32[]{:S(2)}) copy-start(f32[1,6,64]{2,1,0:T(8,128)S(1)} %reduce_window_sum.43) | copy-start | bytes 4612 | tf_op jit(solution)/shard_map/jvp()/while
  162.7 36.7 %copy-start.80 = (f32[6,64]{1,0:T(8,128)}, f32[6,64]{1,0:T(8,128)S(1)}, u32[]{:S(2)}) copy-start(f32[6,64]{1,0:T(8,128)S(1)} %get-tuple-element.2739) | copy-start | bytes 4612 | tf_op jit(solution)/shard_map/jvp()/while
  320.6 28.2 %copy-start.25 = (f32[128,1024]{1,0:T(8,128)}, f32[128,1024]{1,0:T(8,128)S(1)}, u32[]{:S(2)}) copy-start(f32[128,1024]{1,0:T(8,128)S(1)} %get-tuple-element.2183) | copy-start | bytes 1572868
  320.6 28.2 %copy-start.188 = (f32[128]{0:T(128)}, f32[128]{0:T(128)S(1)}, u32[]{:S(2)}) copy-start(f32[128]{0:T(128)S(1)} %fusion.319) | copy-start | bytes 1540
  343.1 6.5 copy-start.89
  348.8 6.7 copy-start.192
  408.0 7.5 copy-start.1
  474.4 7.6 copy-start.1
  520.1 7.4 copy-start.113
  520.1 7.4 copy-start.115
  520.1 7.4 copy-start.117
  544.0 91.3 %all-gather.38.cloned.1.call-start = ((), (), s32[]{:S(2)}) async-start(), calls=%async_computation.16 | async-start | bytes 1310720 | tf_op jit(solution)/shard_map/all_gather | solution.py:240
  544.6 112.0 %all-gather.42.cloned.1.call-start = ((), (), s32[]{:S(2)}) async-start(), calls=%async_computation.22 | async-start | bytes 1966080 | tf_op jit(solution)/shard_map/all_gather | solution.py:241
  545.3 130.0 %all-gather.44.cloned.1.call-start = ((), (), s32[]{:S(2)}) async-start(), calls=%async_computation.23 | async-start | bytes 1310720 | tf_op jit(solution)/shard_map/all_gather | solution.py:248
  545.9 150.6 %all-gather.56.cloned.1.call-start = ((), (), s32[]{:S(2)}) async-start(), calls=%async_computation.33 | async-start | bytes 1966080 | tf_op jit(solution)/shard_map/all_gather | solution.py:246
  546.7 170.9 %all-gather.40.cloned.1.call-start = ((), (), s32[]{:S(2)}) async-start(), calls=%async_computation.20 | async-start | bytes 1966080 | tf_op jit(solution)/shard_map/all_gather | solution.py:247
  547.2 189.1 %all-gather.46.cloned.1.call-start = ((), (), s32[]{:S(2)}) async-start(), calls=%async_computation.25 | async-start | bytes 1310720 | tf_op jit(solution)/shard_map/all_gather | solution.py:242
  547.8 217.0 %all-gather.48.cloned.1.call-start = ((), (), s32[]{:S(2)}) async-start(), calls=%async_computation.26 | async-start | bytes 3604480 | tf_op jit(solution)/shard_map/all_gather | solution.py:249
  548.4 244.8 %all-gather.50.cloned.1.call-start = ((), (), s32[]{:S(2)}) async-start(), calls=%async_computation.28 | async-start | bytes 3604480 | tf_op jit(solution)/shard_map/all_gather | solution.py:250
  549.0 262.4 %all-gather.54.cloned.1.call-start = ((), (), s32[]{:S(2)}) async-start(), calls=%async_computation.31 | async-start | bytes 1310720 | tf_op jit(solution)/shard_map/all_gather | solution.py:251
  549.6 290.4 %all-gather.52.cloned.1.call-start = ((), (), s32[]{:S(2)}) async-start(), calls=%async_computation.30 | async-start | bytes 3604480 | tf_op jit(solution)/shard_map/all_gather | solution.py:243
  550.3 325.5 %all-reduce.44.cloned.1.call-start = ((), (), s32[]{:S(2)}) async-start(), calls=%async_computation.35 | async-start | bytes 249856 | tf_op jit(solution)/shard_map/psum | solution.py:280
  616.6 326.5 %reduce-scatter.11.cloned.1.call-start = ((), (), s32[]{:S(2)}) async-start(), calls=%async_computation.18 | async-start | bytes 884736 | tf_op jit(solution)/shard_map/reduce_scatter | solution.py:271
  635.3 11.0 copy-start.95
  637.7 371.5 %reduce-scatter.9.cloned.1.call-start = ((), (), s32[]{:S(2)}) async-start(), calls=%async_computation.17 | async-start | bytes 884736 | tf_op jit(solution)/shard_map/reduce_scatter | solution.py:270
  647.7 431.1 %reduce-scatter.17.cloned.1.call-start = ((), (), s32[]{:S(2)}) async-start(), calls=%async_computation.24 | async-start | bytes 1769472 | tf_op jit(solution)/shard_map/reduce_scatter | solution.py:274
  678.4 468.7 %reduce-scatter.13.cloned.1.call-start = ((), (), s32[]{:S(2)}) async-start(), calls=%async_computation.19 | async-start | bytes 1769472 | tf_op jit(solution)/shard_map/reduce_scatter | solution.py:272
  699.9 515.6 %reduce-scatter.15.cloned.1.call-start = ((), (), s32[]{:S(2)}) async-start(), calls=%async_computation.21 | async-start | bytes 1769472 | tf_op jit(solution)/shard_map/reduce_scatter | solution.py:273
  720.9 569.9 %reduce-scatter.19.cloned.1.call-start = ((), (), s32[]{:S(2)}) async-start(), calls=%async_computation.27 | async-start | bytes 3244032 | tf_op jit(solution)/shard_map/reduce_scatter | solution.py:275
  769.5 597.1 %reduce-scatter.21.cloned.1.call-start = ((), (), s32[]{:S(2)}) async-start(), calls=%async_computation.29 | async-start | bytes 3244032 | tf_op jit(solution)/shard_map/reduce_scatter | solution.py:276
  798.0 645.0 %reduce-scatter.23.cloned.1.call-start = ((), (), s32[]{:S(2)}) async-start(), calls=%async_computation.32 | async-start | bytes 3244032 | tf_op jit(solution)/shard_map/reduce_scatter | solution.py:277
  (255 other events, 657.7 us)
Sparse Core Ops, SparseCore 0:
  9.6 22.3 all-gather.25
  33.5 19.6 all-gather.21
  54.8 28.4 all-gather.23
  84.7 28.5 all-gather.27
  114.7 28.5 all-gather.29
  144.7 43.8 all-gather.31
  190.2 43.6 all-gather.33
  235.4 43.7 all-gather.35
  544.1 72.3 all-reduce.41
  618.5 16.7 all-gather.37
  636.9 19.6 all-gather.41
  658.6 16.6 all-gather.43
  676.9 19.6 all-gather.55
  697.9 19.6 all-gather.39
  719.6 16.6 all-gather.45
  737.7 27.0 all-gather.47
  766.2 27.0 all-gather.49
  794.7 16.6 all-gather.53
  812.9 27.0 all-gather.51
  842.9 32.9 all-reduce.43
  879.7 63.2 reduce-scatter.10
  946.9 62.2 reduce-scatter.8
  1013.2 65.5 reduce-scatter.16
  1082.7 64.4 reduce-scatter.12
  1151.1 64.3 reduce-scatter.14
  1219.5 71.2 reduce-scatter.18
  1294.8 71.7 reduce-scatter.20
  1370.8 72.2 reduce-scatter.22
